TPU v7x, 128 devices: a whole 4x4x4 slice. The times are simulated.
128 devices in a mesh: cols: 32 (over y, z, core), grp: 4 (over x).
Axes of the slice: x: 4, y: 4, z: 4, core: 2. Of those that a mesh axis runs over, the one named last changes fastest.
Arguments:
- pilot_seed: int32 [16384], P(('cols', 'grp')), may hold values from 0 to 16777215
- delay_shift: int32 [131072], P(('cols', 'grp')), may hold values from 0 to 511
- active_column: int32 [512], replicated, may hold values from 0 to 131071
- channel: bfloat16 [512, 524288], P(None, ('cols', 'grp')), may hold values from -24 to 24
- initial_power: float32 [131072], P(('cols', 'grp')), may hold values from 0.0001 to 4, as said below
- noise_power: float32 [1], replicated, may hold values from 0.5 to 1.5
Outputs:
- powers: float32 [131072], P(('cols', 'grp'))
- gradient: float32 [131072], P(('cols', 'grp'))
Inputs may be any that keep to these rules, and one draw needn't show every extreme that they name: `initial_power`: every entry is positive.
All inputs are finite; a program needn't handle non-finite values.
Results may differ from a plain program's by a relative error of at most 0.0003.
Values sent between devices are 32-bit elements; how exact they have to be, the bound alone decides.
No kernel may reach another device: no remote copies, remote signals or barrier semaphores. Data moves between devices by JAX's collectives and lax.ppermute only.
A program may use at most 64 MiB of HBM per device.

v0:
```python
import math
import jax
import jax.numpy as jnp
from jax import lax
from jax.sharding import PartitionSpec as P

L = 512
DELAYS = 8
ITERS = 2
mult_first = 747796405
mult_second = 289133645
add_first = 1442695041
mult_third = 2073658381
contract_cols = (((1,), (1,)), ((), ()))


def pilot_matrix(seed_list, shifts):
    row_index = jnp.arange(L, dtype=jnp.int32)[:, None]
    offsets = (row_index - shifts[None, :] + L) % L
    hashed = (
        seed_list[None, :] * jnp.int32(mult_first)
        + offsets * jnp.int32(mult_second)
        + jnp.int32(add_first)
    )
    hashed = jnp.bitwise_xor(
        hashed, jnp.bitwise_and(jnp.right_shift(hashed, 15), jnp.int32(131071))
    )
    hashed = hashed * jnp.int32(mult_third)
    hashed = jnp.bitwise_xor(
        hashed, jnp.bitwise_and(jnp.right_shift(hashed, 13), jnp.int32(524287))
    )
    low_bit = jnp.bitwise_and(jnp.right_shift(hashed, 11), jnp.int32(1))
    return (1 - 2 * low_bit).astype(jnp.float32)


def exact_dot(left, right):
    return jnp.dot(left, right, precision=lax.Precision.HIGHEST, preferred_element_type=jnp.float32)


def shards(pilot_seed, delay_shift, active_column, channel, initial_power, noise_power):
    inv_root = 1.0 / math.sqrt(L)
    device_count = lax.axis_size("cols") * lax.axis_size("grp")
    total_samples = channel.shape[1] * device_count
    col_count = delay_shift.shape[0]
    dictionary = pilot_matrix(jnp.repeat(pilot_seed, DELAYS), delay_shift)
    first_col = lax.axis_index(("cols", "grp")) * col_count
    local_col = active_column - first_col
    owned = jnp.logical_and(local_col >= 0, local_col < col_count)
    clipped = jnp.clip(local_col, 0, col_count - 1)
    seeds_here = jnp.where(owned, pilot_seed[clipped // DELAYS], 0)
    shifts_here = jnp.where(owned, delay_shift[clipped], 0)
    seeds_all, shifts_all = lax.psum((seeds_here, shifts_here), ("cols", "grp"))
    active = pilot_matrix(seeds_all, shifts_all).astype(jnp.bfloat16)
    samples = (jnp.dot(active, channel, preferred_element_type=jnp.float32) * inv_root).astype(
        jnp.bfloat16
    )
    cov_part = lax.dot_general(samples, samples, contract_cols, preferred_element_type=jnp.float32)
    identity = jnp.eye(L, dtype=jnp.float32)
    noise_level = noise_power[0]

    def weighted(powers):
        return dictionary * (powers / L)[None, :]

    def model_part(powers):
        return lax.dot_general(
            weighted(powers),
            dictionary,
            contract_cols,
            precision=lax.Precision.HIGHEST,
            preferred_element_type=jnp.float32,
        )

    cov_sum, first_model = lax.psum((cov_part, model_part(initial_power)), ("cols", "grp"))
    sample_cov = cov_sum / total_samples + noise_level * identity
    powers = initial_power
    gradient = jnp.zeros_like(initial_power)
    summed = first_model
    for iteration in range(ITERS):
        if iteration > 0:
            model_summed = lax.psum(model_part(powers), ("cols", "grp"))
            summed = model_summed
        model_cov = summed + noise_level * identity
        factor = jnp.linalg.cholesky(model_cov)
        invert_result = jax.scipy.linalg.cho_solve((factor, True), identity)
        mapped = exact_dot(invert_result, dictionary)
        weighed = exact_dot(sample_cov, mapped)
        result = (jnp.sum(dictionary * mapped, axis=0) - jnp.sum(mapped * weighed, axis=0)) / L
        gradient = result
        powers = jnp.maximum(powers - gradient, 0.0)
    return (powers, gradient)


def solution(mesh):
    placed = (
        P(("cols", "grp")),
        P(("cols", "grp")),
        P(),
        P(None, ("cols", "grp")),
        P(("cols", "grp")),
        P(),
    )
    return jax.shard_map(
        shards,
        mesh=mesh,
        in_specs=placed,
        out_specs=(P(("cols", "grp")), P(("cols", "grp"))),
        check_vma=False,
    )
```

profile of v0, /device:TPU:1, one launch (start us, length us, event | category | flops | bytes accessed | tf_op | source)
XLA Modules:
  0.0 734.1 jit_solution(4290212688632799999)
XLA Ops:
  8.6 3.5 gather_fusion
  12.1 2.3 gather_fusion.1
  14.4 68.8 %all-reduce.1 = (s32[512]{0:T(512)S(1)}, s32[512]{0:T(512)S(1)}) all-reduce(s32[512]{0:T(512)S(1)} %broadcast_select_fusion, s32[512]{0:T(512)S(1)} %get-tuple-element.42), channel_id=1, replica_groups=mesh['cols'=32,'grp'=4] {'cols','grp'}, use_global_device_ids=true, to_apply=%region_11.14 | all-reduce | flops 1024 | bytes 8192 | tf_op jit(solution)/shard_map/psum | solution.py:52
  83.5 8.0 %fusion.2 = f32[512,512]{0,1:T(8,128)} fusion(f32[1024]{0:T(1024)S(1)} %broadcast_multiply_fusion.1, s32[1024]{0:T(1024)S(1)} %copy-done, s32[1024]{0:T(1024)S(1)} %mul.110), kind=kOutput, calls=%fused_computation.9 | convolution fusion | flops 3251109888 | bytes 1060864 | tf_op jit(solution)/shard_map/dot_general | solution.py:65
  91.5 13.1 %fusion.73 = f32[512,512]{0,1:T(8,128)} fusion(bf16[512,4096]{1,0:T(8,128)(2,1)} %param.12, s32[512]{0:T(512)S(1)} %get-tuple-element.36, s32[512]{0:T(512)S(1)} %broadcast_multiply_fusion.2), kind=kOutput, calls=%fused_computation.123 | convolution fusion | flops 4306763776 | bytes 5246976 | tf_op jit(solution)/shard_map/dot_general | solution.py:57
  105.4 146.8 %all-reduce.8.cloned.1.call-done = (f32[512,512]{0,1:T(8,128)}, f32[512,512]{0,1:T(8,128)}) async-done(((f32[512,512]{0,1:T(8,128)}, f32[512,512]{0,1:T(8,128)}), (f32[512,512]{0,1:T(8,128)}, f32[512,512]{0,1:T(8,128)})) %all-reduce.8.cloned.1.call-update) | async-done | bytes 2097168 | tf_op jit(solution)/shard_map/psum | solution.py:73
  254.9 1.5 fusion.33
  257.5 11.7 %cholesky.286 = f32[128,128]{1,0:T(8,128)S(1)} custom-call(f32[128,128]{1,0:T(8,128)S(1)} %cholesky.426), custom_call_target="Cholesky" | custom-call | tf_op jit(solution)/shard_map/jit(cholesky)/cholesky | solution.py:83
  269.2 9.8 %custom-call.29 = f32[1,128,128]{1,2,0:T(8,128)S(1)} custom-call(f32[1,128,128]{2,1,0:T(8,128)S(1)} %get-tuple-element.67), custom_call_target="InvertDiagBlocksLowerTriangular" | custom-call | tf_op jit(solution)/shard_map/jit(cholesky)/cholesky | solution.py:83
  281.7 11.7 %cholesky.305 = f32[128,128]{1,0:T(8,128)S(1)} custom-call(f32[128,128]{1,0:T(8,128)S(1)} %cholesky.430), custom_call_target="Cholesky" | custom-call | tf_op jit(solution)/shard_map/jit(cholesky)/cholesky | solution.py:83
  293.4 10.0 %custom-call.30 = f32[1,128,128]{1,2,0:T(8,128)S(1)} custom-call(f32[1,128,128]{2,1,0:T(8,128)S(1)} %get-tuple-element.64), custom_call_target="InvertDiagBlocksLowerTriangular" | custom-call | tf_op jit(solution)/shard_map/jit(cholesky)/cholesky | solution.py:83
  305.0 11.7 %cholesky.326 = f32[128,128]{1,0:T(8,128)S(1)} custom-call(f32[128,128]{1,0:T(8,128)S(1)} %cholesky.435), custom_call_target="Cholesky" | custom-call | tf_op jit(solution)/shard_map/jit(cholesky)/cholesky | solution.py:83
  317.4 9.8 %custom-call.31 = f32[1,128,128]{1,2,0:T(8,128)S(1)} custom-call(f32[1,128,128]{2,1,0:T(8,128)S(1)} %get-tuple-element.61), custom_call_target="InvertDiagBlocksLowerTriangular" | custom-call | tf_op jit(solution)/shard_map/jit(cholesky)/cholesky | solution.py:83
  328.6 11.7 %cholesky.343 = f32[128,128]{1,0:T(8,128)S(1)} custom-call(f32[128,128]{1,0:T(8,128)S(1)} %convolution_subtract_fusion.17), custom_call_target="Cholesky" | custom-call | tf_op jit(solution)/shard_map/jit(cholesky)/cholesky | solution.py:83
  344.8 8.1 %while.4 = (s32[]{:T(128)}, f32[512,512]{1,0:T(8,128)S(1)}, s32[4,2]{0,1:T(2,128)S(1)}, f32[4,128,128]{2,1,0:T(8,128)S(1)}, s32[]{:T(128)}) while((s32[]{:T(128)}, f32[512,512]{1,0:T(8,128)S(1)}, s32[4,2]{0,1:T(2,128)S(1)}, f32[4,128,128]{2,1,0:T(8,128)S(1)}, s32[]{:T(128)}) %tuple.60), condition=%wide.while_cond, body=%wide.while_body.sunk | while | flops 2 | bytes 131181 | solution.py:84
  353.0 39.3 %custom-call.32 = f32[4,128,128]{1,2,0:T(8,128)S(1)} custom-call(f32[4,128,128]{2,1,0:T(8,128)S(1)} %get-tuple-element.18), custom_call_target="InvertDiagBlocksLowerTriangular" | custom-call | tf_op jit(solution)/shard_map/jit(_cho_solve)/triangular_solve | solution.py:84
  400.2 7.3 multiply_reduce_fusion.3
  407.5 3.6 multiply_reduce_fusion.2
  411.2 8.0 %fusion = f32[512,512]{0,1:T(8,128)} fusion(f32[1024]{0:T(1024)S(1)} %broadcast_multiply_fusion, s32[1024]{0:T(1024)S(1)} %copy-done, s32[1024]{0:T(1024)S(1)} %mul.110), kind=kOutput, calls=%fused_computation.7 | convolution fusion | flops 3251109888 | bytes 1060864 | tf_op jit(solution)/shard_map/dot_general | solution.py:65
  419.2 146.9 %all-reduce.6.cloned.1.call-done = f32[512,512]{0,1:T(8,128)} async-done(((f32[512,512]{0,1:T(8,128)}), f32[512,512]{0,1:T(8,128)}) %all-reduce.6.cloned.1.call-update) | async-done | bytes 1048592 | tf_op jit(solution)/shard_map/psum | solution.py:80
  567.5 1.7 copy.17
  571.8 11.7 %cholesky.358 = f32[128,128]{1,0:T(8,128)S(1)} custom-call(f32[128,128]{1,0:T(8,128)S(1)} %cholesky.439), custom_call_target="Cholesky" | custom-call | tf_op jit(solution)/shard_map/jit(cholesky)/cholesky | solution.py:83
  583.7 9.8 %custom-call.33 = f32[1,128,128]{1,2,0:T(8,128)S(1)} custom-call(f32[1,128,128]{2,1,0:T(8,128)S(1)} %get-tuple-element.57), custom_call_target="InvertDiagBlocksLowerTriangular" | custom-call | tf_op jit(solution)/shard_map/jit(cholesky)/cholesky | solution.py:83
  596.0 11.7 %cholesky.377 = f32[128,128]{1,0:T(8,128)S(1)} custom-call(f32[128,128]{1,0:T(8,128)S(1)} %cholesky.443), custom_call_target="Cholesky" | custom-call | tf_op jit(solution)/shard_map/jit(cholesky)/cholesky | solution.py:83
  609.0 10.0 %custom-call.34 = f32[1,128,128]{1,2,0:T(8,128)S(1)} custom-call(f32[1,128,128]{2,1,0:T(8,128)S(1)} %get-tuple-element.54), custom_call_target="InvertDiagBlocksLowerTriangular" | custom-call | tf_op jit(solution)/shard_map/jit(cholesky)/cholesky | solution.py:83
  620.6 11.7 %cholesky.398 = f32[128,128]{1,0:T(8,128)S(1)} custom-call(f32[128,128]{1,0:T(8,128)S(1)} %cholesky.448), custom_call_target="Cholesky" | custom-call | tf_op jit(solution)/shard_map/jit(cholesky)/cholesky | solution.py:83
  633.0 9.8 %custom-call.35 = f32[1,128,128]{1,2,0:T(8,128)S(1)} custom-call(f32[1,128,128]{2,1,0:T(8,128)S(1)} %get-tuple-element.51), custom_call_target="InvertDiagBlocksLowerTriangular" | custom-call | tf_op jit(solution)/shard_map/jit(cholesky)/cholesky | solution.py:83
  644.3 11.7 %cholesky.415 = f32[128,128]{1,0:T(8,128)S(1)} custom-call(f32[128,128]{1,0:T(8,128)S(1)} %convolution_subtract_fusion.16), custom_call_target="Cholesky" | custom-call | tf_op jit(solution)/shard_map/jit(cholesky)/cholesky | solution.py:83
  659.5 8.5 %while.5 = (s32[]{:T(128)}, f32[512,512]{1,0:T(8,128)S(1)}, s32[4,2]{0,1:T(2,128)S(1)}, f32[4,128,128]{2,1,0:T(8,128)S(1)}, s32[]{:T(128)}) while((s32[]{:T(128)}, f32[512,512]{1,0:T(8,128)S(1)}, s32[4,2]{0,1:T(2,128)S(1)}, f32[4,128,128]{2,1,0:T(8,128)S(1)}, s32[]{:T(128)}) %tuple.71), condition=%wide.while_cond.clone, body=%wide.while_body.clone.sunk | while | flops 2 | bytes 131181 | solution.py:84
  667.9 39.5 %custom-call.36 = f32[4,128,128]{1,2,0:T(8,128)S(1)} custom-call(f32[4,128,128]{2,1,0:T(8,128)S(1)} %get-tuple-element.19), custom_call_target="InvertDiagBlocksLowerTriangular" | custom-call | tf_op jit(solution)/shard_map/jit(_cho_solve)/triangular_solve | solution.py:84
  715.4 7.4 %multiply_reduce_fusion.1 = (f32[1024]{0:T(1024)S(1)}, f32[512,1024]{1,0:T(8,128)S(1)}) fusion(s32[1024]{0:T(1024)S(1)} %copy-done, s32[1024]{0:T(1024)S(1)} %mul.110, f32[128,512]{1,0:T(8,128)S(1)} %fusion.154, f32[128,512]{1,0:T(8,128)S(1)} %fusion.152, f32[128,512]{1,0:T(8,128)S(1)} %fusion.150, f32[128,512]{1,0:T(8,128)S(1)} %fusion.149), kind=kOutput, calls=%fused_computation.19 | convolution fusion | flops 3252419584 | bytes 3158016 | tf_op jit(solution)/shard_map/dot_general | solution.py:37
  722.7 3.6 multiply_reduce_fusion
  (132 shorter events, 59.0 us)
Async XLA Ops:
  7.2 4.9 copy-start.6
  7.2 4.9 copy-start
  7.2 245.0 %all-reduce.8.cloned.1.call-start = ((), (), s32[]{:S(2)}) async-start(), calls=%async_computation.1 | async-start | bytes 4194304 | tf_op jit(solution)/shard_map/psum | solution.py:73
  8.6 74.8 %copy-start.5 = (f32[1024]{0:T(1024)S(1)}, f32[1024]{0:T(1024)}, u32[]{:S(2)}) copy-start(f32[1024]{0:T(1024)} %param.13) | copy-start | bytes 12292
  104.6 461.5 %all-reduce.6.cloned.1.call-start = ((), (), s32[]{:S(2)}) async-start(), calls=%async_computation | async-start | bytes 2097152 | tf_op jit(solution)/shard_map/psum | solution.py:80
  252.2 2.8 copy-start.1
  256.4 1.0 copy-start.4
  400.2 7.3 copy-start.7
  566.1 3.2 copy-start.2
  570.7 1.0 copy-start.3
  715.4 7.4 %copy-start.8 = (f32[512,512]{0,1:T(8,128)S(1)}, f32[512,512]{0,1:T(8,128)}, u32[]{:S(2)}) copy-start(f32[512,512]{0,1:T(8,128)} %get-tuple-element.39) | copy-start | bytes 3145732
Sparse Core Ops, SparseCore 0:
  104.7 147.4 all-reduce.7
  419.3 146.7 all-reduce.5
where the time goes:
time: 737 us; the launch traced here: 734 us
  waiting for transfers between devices  294 us (40%)
  other arithmetic  245 us (33%)
  matrix products  77.5 us (11%)
  blocking collectives  68.8 us (9%)
  local copies, waits for them, and re-layouts  27.8 us (4%)
  between operations  20.7 us (3%)
    another operation x29, other arithmetic, shards(): factor = jnp.linalg.cholesky(model_cov)  158 us
    psum x1, waiting for transfers between devices, shards(): model_summed = lax.psum(model_part(powers), ('cols', 'grp'))  147 us
    psum x1, waiting for transfers between devices, shards(): lax.psum((cov_part, model_part(initial_power)), ('cols', 'grp'))  147 us
    another operation x5, other arithmetic, shards(): invert_result = jax.scipy.linalg.cho_solve((factor, True), identity)  79.1 us
    psum x1, blocking collectives, shards(): seeds_all, shifts_all = lax.psum((seeds_here, shifts_here), ('cols', 'grp'))  68.8 us
    dot_general x4, matrix products, exact_dot(): jnp.dot(left, right, precision=lax.Precision.HIGHEST, preferred_element_t...  21.9 us
    another operation x27, local copies, waits for them, and re-layouts, shards(): invert_result = jax.scipy.linalg.cho_solve((factor, True), identity)  16.5 us
    dot_general x2, matrix products, model_part(): lax.dot_general(weighted(powers), dictionary, contract_cols, precision=la...  16 us
  transfers between devices with their start and end apart: 2, of which 2 were waited for; matrix products, arithmetic and copies ran while one was open for 0% of the time, Pallas kernels for 0%

commit v1 on v0

--- a/solution.py
+++ b/solution.py
@@ -12,6 +12,11 @@
 add_first = 1442695041
 mult_third = 2073658381
 contract_cols = (((1,), (1,)), ((), ()))
+
+
+def by_each_axis(value, axis_one, axis_two):
+    half = lax.psum(value, axis_one)
+    return lax.psum(half, axis_two)
 
 
 def pilot_matrix(seed_list, shifts):
@@ -49,7 +54,7 @@
     clipped = jnp.clip(local_col, 0, col_count - 1)
     seeds_here = jnp.where(owned, pilot_seed[clipped // DELAYS], 0)
     shifts_here = jnp.where(owned, delay_shift[clipped], 0)
-    seeds_all, shifts_all = lax.psum((seeds_here, shifts_here), ("cols", "grp"))
+    seeds_all, shifts_all = by_each_axis((seeds_here, shifts_here), "cols", "grp")
     active = pilot_matrix(seeds_all, shifts_all).astype(jnp.bfloat16)
     samples = (jnp.dot(active, channel, preferred_element_type=jnp.float32) * inv_root).astype(
         jnp.bfloat16

time: 737 us -> 702 us (0.953); the launches traced: 734 us -> 691 us
  blocking collectives: 68.8 us -> 22.9 us
    psum x1 -> x2, blocking collectives: 68.8 us -> 22.9 us  [the longest x1 15.7 us: by_each_axis(): half = lax.psum(value, axis_one)]
where the time goes in v1:
time: 702 us; the launch traced here: 691 us
  waiting for transfers between devices  297 us (42%)
  other arithmetic  245 us (35%)
  matrix products  77.4 us (11%)
  local copies, waits for them, and re-layouts  27.8 us (4%)
  blocking collectives  22.9 us (3%)
  between operations  20.9 us (3%)
    another operation x29, other arithmetic, shards(): factor = jnp.linalg.cholesky(model_cov)  158 us
    psum x1, waiting for transfers between devices, shards(): lax.psum((cov_part, model_part(initial_power)), ('cols', 'grp'))  150 us
    psum x1, waiting for transfers between devices, shards(): model_summed = lax.psum(model_part(powers), ('cols', 'grp'))  147 us
    another operation x5, other arithmetic, shards(): invert_result = jax.scipy.linalg.cho_solve((factor, True), identity)  79.1 us
    dot_general x4, matrix products, exact_dot(): jnp.dot(left, right, precision=lax.Precision.HIGHEST, preferred_element_t...  21.8 us
    another operation x27, local copies, waits for them, and re-layouts, shards(): invert_result = jax.scipy.linalg.cho_solve((factor, True), identity)  16.5 us
    dot_general x2, matrix products, model_part(): lax.dot_general(weighted(powers), dictionary, contract_cols, precision=la...  16 us
    psum x1, blocking collectives, by_each_axis(): half = lax.psum(value, axis_one)  15.7 us
  transfers between devices with their start and end apart: 2, of which 2 were waited for; matrix products, arithmetic and copies ran while one was open for 0% of the time, Pallas kernels for 0%

profile of v1, /device:TPU:1, one launch (start us, length us, event | category | flops | bytes accessed | tf_op | source)
XLA Modules:
  0.0 691.4 jit_solution(5540285398355207402)
XLA Ops:
  8.6 3.5 gather_fusion
  12.1 2.3 gather_fusion.1
  14.4 15.7 %all-reduce.1 = (s32[512]{0:T(512)S(1)}, s32[512]{0:T(512)S(1)}) all-reduce(s32[512]{0:T(512)S(1)} %broadcast_select_fusion, s32[512]{0:T(512)S(1)} %get-tuple-element.44), channel_id=1, replica_groups=mesh['cols'=32,'grp'=4] {'cols'}, use_global_device_ids=true, to_apply=%region_12.15 | all-reduce | flops 1024 | bytes 8192 | tf_op jit(solution)/shard_map/psum | solution.py:18
  30.2 7.2 %all-reduce.2 = (s32[512]{0:T(512)S(1)}, s32[512]{0:T(512)S(1)}) all-reduce(s32[512]{0:T(512)S(1)} %get-tuple-element.36, s32[512]{0:T(512)S(1)} %get-tuple-element.37), channel_id=1, replica_groups=mesh['cols'=32,'grp'=4] {'grp'}, use_global_device_ids=true, to_apply=%region_13.16 | all-reduce | flops 1024 | bytes 8192 | tf_op jit(solution)/shard_map/psum | solution.py:19
  37.5 8.0 %fusion.2 = f32[512,512]{0,1:T(8,128)} fusion(f32[1024]{0:T(1024)S(1)} %broadcast_multiply_fusion.1, s32[1024]{0:T(1024)S(1)} %copy-done, s32[1024]{0:T(1024)S(1)} %mul.110), kind=kOutput, calls=%fused_computation.9 | convolution fusion | flops 3251109888 | bytes 1060864 | tf_op jit(solution)/shard_map/dot_general | solution.py:70
  45.5 13.0 %fusion.73 = f32[512,512]{0,1:T(8,128)} fusion(bf16[512,4096]{1,0:T(8,128)(2,1)} %param.12, s32[512]{0:T(512)S(1)} %get-tuple-element.38, s32[512]{0:T(512)S(1)} %broadcast_multiply_fusion.2), kind=kOutput, calls=%fused_computation.123 | convolution fusion | flops 4306763776 | bytes 5246976 | tf_op jit(solution)/shard_map/dot_general | solution.py:62
  59.4 150.0 %all-reduce.9.cloned.1.call-done = (f32[512,512]{0,1:T(8,128)}, f32[512,512]{0,1:T(8,128)}) async-done(((f32[512,512]{0,1:T(8,128)}, f32[512,512]{0,1:T(8,128)}), (f32[512,512]{0,1:T(8,128)}, f32[512,512]{0,1:T(8,128)})) %all-reduce.9.cloned.1.call-update) | async-done | bytes 2097168 | tf_op jit(solution)/shard_map/psum | solution.py:78
  214.6 11.7 %cholesky.286 = f32[128,128]{1,0:T(8,128)S(1)} custom-call(f32[128,128]{1,0:T(8,128)S(1)} %cholesky.426), custom_call_target="Cholesky" | custom-call | tf_op jit(solution)/shard_map/jit(cholesky)/cholesky | solution.py:88
  226.5 9.8 %custom-call.29 = f32[1,128,128]{1,2,0:T(8,128)S(1)} custom-call(f32[1,128,128]{2,1,0:T(8,128)S(1)} %get-tuple-element.69), custom_call_target="InvertDiagBlocksLowerTriangular" | custom-call | tf_op jit(solution)/shard_map/jit(cholesky)/cholesky | solution.py:88
  238.8 11.7 %cholesky.305 = f32[128,128]{1,0:T(8,128)S(1)} custom-call(f32[128,128]{1,0:T(8,128)S(1)} %cholesky.430), custom_call_target="Cholesky" | custom-call | tf_op jit(solution)/shard_map/jit(cholesky)/cholesky | solution.py:88
  250.6 10.0 %custom-call.30 = f32[1,128,128]{1,2,0:T(8,128)S(1)} custom-call(f32[1,128,128]{2,1,0:T(8,128)S(1)} %get-tuple-element.66), custom_call_target="InvertDiagBlocksLowerTriangular" | custom-call | tf_op jit(solution)/shard_map/jit(cholesky)/cholesky | solution.py:88
  262.1 11.7 %cholesky.326 = f32[128,128]{1,0:T(8,128)S(1)} custom-call(f32[128,128]{1,0:T(8,128)S(1)} %cholesky.435), custom_call_target="Cholesky" | custom-call | tf_op jit(solution)/shard_map/jit(cholesky)/cholesky | solution.py:88
  274.5 9.8 %custom-call.31 = f32[1,128,128]{1,2,0:T(8,128)S(1)} custom-call(f32[1,128,128]{2,1,0:T(8,128)S(1)} %get-tuple-element.63), custom_call_target="InvertDiagBlocksLowerTriangular" | custom-call | tf_op jit(solution)/shard_map/jit(cholesky)/cholesky | solution.py:88
  285.8 11.7 %cholesky.343 = f32[128,128]{1,0:T(8,128)S(1)} custom-call(f32[128,128]{1,0:T(8,128)S(1)} %convolution_subtract_fusion.17), custom_call_target="Cholesky" | custom-call | tf_op jit(solution)/shard_map/jit(cholesky)/cholesky | solution.py:88
  302.0 8.1 %while.4 = (s32[]{:T(128)}, f32[512,512]{1,0:T(8,128)S(1)}, s32[4,2]{0,1:T(2,128)S(1)}, f32[4,128,128]{2,1,0:T(8,128)S(1)}, s32[]{:T(128)}) while((s32[]{:T(128)}, f32[512,512]{1,0:T(8,128)S(1)}, s32[4,2]{0,1:T(2,128)S(1)}, f32[4,128,128]{2,1,0:T(8,128)S(1)}, s32[]{:T(128)}) %tuple.60), condition=%wide.while_cond, body=%wide.while_body.sunk | while | flops 2 | bytes 131181 | solution.py:89
  310.1 39.3 %custom-call.32 = f32[4,128,128]{1,2,0:T(8,128)S(1)} custom-call(f32[4,128,128]{2,1,0:T(8,128)S(1)} %get-tuple-element.18), custom_call_target="InvertDiagBlocksLowerTriangular" | custom-call | tf_op jit(solution)/shard_map/jit(_cho_solve)/triangular_solve | solution.py:89
  357.4 7.3 %multiply_reduce_fusion.3 = (f32[1024]{0:T(1024)S(1)}, f32[512,1024]{1,0:T(8,128)S(1)}) fusion(s32[1024]{0:T(1024)S(1)} %copy-done, s32[1024]{0:T(1024)S(1)} %mul.110, f32[128,512]{1,0:T(8,128)S(1)} %fusion.147, f32[128,512]{1,0:T(8,128)S(1)} %fusion.145, f32[128,512]{1,0:T(8,128)S(1)} %fusion.143, f32[128,512]{1,0:T(8,128)S(1)} %fusion.142), kind=kOutput, calls=%fused_computation.21 | convolution fusion | flops 3252419584 | bytes 3158016 | tf_op jit(solution)/shard_map/dot_general | solution.py:42
  364.7 3.7 multiply_reduce_fusion.2
  368.3 8.0 %fusion = f32[512,512]{0,1:T(8,128)} fusion(f32[1024]{0:T(1024)S(1)} %broadcast_multiply_fusion, s32[1024]{0:T(1024)S(1)} %copy-done, s32[1024]{0:T(1024)S(1)} %mul.110), kind=kOutput, calls=%fused_computation.7 | convolution fusion | flops 3251109888 | bytes 1060864 | tf_op jit(solution)/shard_map/dot_general | solution.py:70
  376.4 147.0 %all-reduce.7.cloned.1.call-done = f32[512,512]{0,1:T(8,128)} async-done(((f32[512,512]{0,1:T(8,128)}), f32[512,512]{0,1:T(8,128)}) %all-reduce.7.cloned.1.call-update) | async-done | bytes 1048592 | tf_op jit(solution)/shard_map/psum | solution.py:85
  524.8 1.7 copy.17
  529.0 11.7 %cholesky.358 = f32[128,128]{1,0:T(8,128)S(1)} custom-call(f32[128,128]{1,0:T(8,128)S(1)} %cholesky.439), custom_call_target="Cholesky" | custom-call | tf_op jit(solution)/shard_map/jit(cholesky)/cholesky | solution.py:88
  540.9 9.8 %custom-call.33 = f32[1,128,128]{1,2,0:T(8,128)S(1)} custom-call(f32[1,128,128]{2,1,0:T(8,128)S(1)} %get-tuple-element.59), custom_call_target="InvertDiagBlocksLowerTriangular" | custom-call | tf_op jit(solution)/shard_map/jit(cholesky)/cholesky | solution.py:88
  553.2 11.7 %cholesky.377 = f32[128,128]{1,0:T(8,128)S(1)} custom-call(f32[128,128]{1,0:T(8,128)S(1)} %cholesky.443), custom_call_target="Cholesky" | custom-call | tf_op jit(solution)/shard_map/jit(cholesky)/cholesky | solution.py:88
  566.3 10.0 %custom-call.34 = f32[1,128,128]{1,2,0:T(8,128)S(1)} custom-call(f32[1,128,128]{2,1,0:T(8,128)S(1)} %get-tuple-element.56), custom_call_target="InvertDiagBlocksLowerTriangular" | custom-call | tf_op jit(solution)/shard_map/jit(cholesky)/cholesky | solution.py:88
  577.8 11.7 %cholesky.398 = f32[128,128]{1,0:T(8,128)S(1)} custom-call(f32[128,128]{1,0:T(8,128)S(1)} %cholesky.448), custom_call_target="Cholesky" | custom-call | tf_op jit(solution)/shard_map/jit(cholesky)/cholesky | solution.py:88
  590.2 9.8 %custom-call.35 = f32[1,128,128]{1,2,0:T(8,128)S(1)} custom-call(f32[1,128,128]{2,1,0:T(8,128)S(1)} %get-tuple-element.53), custom_call_target="InvertDiagBlocksLowerTriangular" | custom-call | tf_op jit(solution)/shard_map/jit(cholesky)/cholesky | solution.py:88
  601.5 11.7 %cholesky.415 = f32[128,128]{1,0:T(8,128)S(1)} custom-call(f32[128,128]{1,0:T(8,128)S(1)} %convolution_subtract_fusion.16), custom_call_target="Cholesky" | custom-call | tf_op jit(solution)/shard_map/jit(cholesky)/cholesky | solution.py:88
  616.7 8.5 %while.5 = (s32[]{:T(128)}, f32[512,512]{1,0:T(8,128)S(1)}, s32[4,2]{0,1:T(2,128)S(1)}, f32[4,128,128]{2,1,0:T(8,128)S(1)}, s32[]{:T(128)}) while((s32[]{:T(128)}, f32[512,512]{1,0:T(8,128)S(1)}, s32[4,2]{0,1:T(2,128)S(1)}, f32[4,128,128]{2,1,0:T(8,128)S(1)}, s32[]{:T(128)}) %tuple.71), condition=%wide.while_cond.clone, body=%wide.while_body.clone.sunk | while | flops 2 | bytes 131181 | solution.py:89
  625.2 39.5 %custom-call.36 = f32[4,128,128]{1,2,0:T(8,128)S(1)} custom-call(f32[4,128,128]{2,1,0:T(8,128)S(1)} %get-tuple-element.19), custom_call_target="InvertDiagBlocksLowerTriangular" | custom-call | tf_op jit(solution)/shard_map/jit(_cho_solve)/triangular_solve | solution.py:89
  672.6 7.3 %multiply_reduce_fusion.1 = (f32[1024]{0:T(1024)S(1)}, f32[512,1024]{1,0:T(8,128)S(1)}) fusion(s32[1024]{0:T(1024)S(1)} %copy-done, s32[1024]{0:T(1024)S(1)} %mul.110, f32[128,512]{1,0:T(8,128)S(1)} %fusion.154, f32[128,512]{1,0:T(8,128)S(1)} %fusion.152, f32[128,512]{1,0:T(8,128)S(1)} %fusion.150, f32[128,512]{1,0:T(8,128)S(1)} %fusion.149), kind=kOutput, calls=%fused_computation.19 | convolution fusion | flops 3252419584 | bytes 3158016 | tf_op jit(solution)/shard_map/dot_general | solution.py:42
  680.0 3.5 multiply_reduce_fusion
  (133 shorter events, 60.6 us)
Async XLA Ops:
  7.2 4.9 copy-start.6
  7.2 4.9 copy-start
  7.2 202.1 %all-reduce.9.cloned.1.call-start = ((), (), s32[]{:S(2)}) async-start(), calls=%async_computation.1 | async-start | bytes 4194304 | tf_op jit(solution)/shard_map/psum | solution.py:78
  8.6 28.9 %copy-start.5 = (f32[1024]{0:T(1024)S(1)}, f32[1024]{0:T(1024)}, u32[]{:S(2)}) copy-start(f32[1024]{0:T(1024)} %param.13) | copy-start | bytes 12292
  58.5 464.8 %all-reduce.7.cloned.1.call-start = ((), (), s32[]{:S(2)}) async-start(), calls=%async_computation | async-start | bytes 2097152 | tf_op jit(solution)/shard_map/psum | solution.py:85
  209.3 2.8 copy-start.1
  213.6 1.0 copy-start.4
  357.3 7.3 %copy-start.7 = (f32[512,512]{0,1:T(8,128)S(1)}, f32[512,512]{0,1:T(8,128)}, u32[]{:S(2)}) copy-start(f32[512,512]{0,1:T(8,128)} %get-tuple-element.41) | copy-start | bytes 3145732
  523.3 3.2 copy-start.2
  528.0 1.0 copy-start.3
  672.6 7.4 %copy-start.8 = (f32[512,512]{0,1:T(8,128)S(1)}, f32[512,512]{0,1:T(8,128)}, u32[]{:S(2)}) copy-start(f32[512,512]{0,1:T(8,128)} %get-tuple-element.41) | copy-start | bytes 3145732
Sparse Core Ops, SparseCore 0:
  58.7 150.6 all-reduce.8
  376.5 146.7 all-reduce.6
